TPU v7x, 256 devices: a whole 4x4x8 slice. The times are simulated.
256 devices in a mesh: context: 16 (over z, core), heads: 16 (over x, y).
Axes of the slice: x: 4, y: 4, z: 8, core: 2. Of those that a mesh axis runs over, the one named last changes fastest.
Arguments:
- main_query: bfloat16 [256, 128, 576], P('context', 'heads'), may hold values from -6 to 6
- latent_keys: bfloat16 [32768, 576], P('context'), may hold values from -6 to 6
- head_lse: float32 [256, 128], P(None, 'heads'), may hold values from 4 to 8
- lengths: int32 [256], replicated, may hold values from 1 to 32768, as said below
- index_query: bfloat16 [256, 64, 128], P('heads'), may hold values from -256 to 256
- index_key: bfloat16 [32768, 128], P('context'), may hold values from -8 to 8
- index_weight: float32 [256, 64], P('heads'), may hold values from -2.4 to 2.4
Outputs:
- grad_index_query: float32 [256, 64, 128], P('heads', 'context')
- grad_index_key: float32 [32768, 128], P(('context', 'heads'))
Inputs may be any that keep to these rules, and one draw needn't show every extreme that they name: Query rows come in blocks of 16 consecutive rows whose lengths rise by one from row to row; some block ends at the last key.
All inputs are finite; a program needn't handle non-finite values.
Results may differ from a plain program's by a relative error of at most 0.0029.
Values may be sent and summed in bfloat16 or wider, within the bound.
A program may use at most 64 MiB of HBM per device.

v0:
```python
import math
import jax
import jax.numpy as jnp
from jax import lax
from jax.sharding import PartitionSpec as P

main_scale = 192.0 ** (-0.5)
loss_scale = 64.0
masked_low = -1e30


def head_mass(queries, lse_rows, len_rows, latent, first_key):
    row_count = queries.shape[0]
    block_rows = math.gcd(row_count, 64)
    steps_count = row_count // block_rows
    key_pos = first_key + jnp.arange(latent.shape[0], dtype=jnp.int32)

    def one_block(inputs):
        query_block, lse_block, len_block = inputs
        scores = (
            jnp.einsum("rhd,sd->rhs", query_block, latent, preferred_element_type=jnp.float32)
            * main_scale
        )
        summed = jnp.sum(jnp.exp(scores - lse_block[:, :, None]), axis=1)
        return jnp.where(key_pos[None, :] < len_block[:, None], summed, 0.0)

    stacked = lax.map(
        one_block,
        (
            queries.reshape((steps_count, block_rows) + queries.shape[1:]),
            lse_rows.reshape(steps_count, block_rows, lse_rows.shape[1]),
            len_rows.reshape(steps_count, block_rows),
        ),
    )
    return stacked.reshape(row_count, latent.shape[0])


def on_device(main_query, latent_keys, head_lse, lengths, index_query, index_key, index_weight):
    key_count = latent_keys.shape[0]
    first_key = lax.axis_index("context") * key_count
    own_rows = index_query.shape[0]
    row_first = lax.axis_index("heads") * own_rows
    partial_mass = head_mass(
        lax.all_gather(main_query, "context", axis=0, tiled=True),
        head_lse,
        lengths,
        latent_keys,
        first_key,
    )
    summed_mass = lax.psum(partial_mass, "heads")
    row_mass = lax.dynamic_slice_in_dim(summed_mass, row_first, own_rows, 0)
    own_len = lax.dynamic_slice_in_dim(lengths, row_first, own_rows, 0)
    visible = (first_key + jnp.arange(key_count, dtype=jnp.int32))[None, :] < own_len[:, None]
    heads_count = index_query.shape[1]
    width = index_query.shape[2]
    index_scale = width ** (-0.5)
    flat_query = index_query.reshape(own_rows * heads_count, width)
    block_keys = math.gcd(key_count, 512)
    block_total = key_count // block_keys
    key_blocks = index_key.reshape(block_total, block_keys, width)

    def block_dots(key_block):
        products = lax.dot_general(
            flat_query, key_block, (((1,), (1,)), ((), ())), preferred_element_type=jnp.float32
        )
        return products.reshape(own_rows, heads_count, key_block.shape[0])

    def block_logits(key_block):
        return (
            jnp.einsum(
                "tj,tjs->ts",
                index_weight,
                jax.nn.relu(block_dots(key_block)),
                precision=lax.Precision.HIGHEST,
            )
            * index_scale
        )

    logits = jnp.moveaxis(lax.map(block_logits, key_blocks), 0, 1).reshape(own_rows, key_count)
    local_top = jnp.max(jnp.where(visible, logits, masked_low), axis=1)
    mass_local = jnp.sum(row_mass, axis=1)
    top = lax.pmax(local_top, "context")
    weights_exp = jnp.where(visible, jnp.exp(logits - top[:, None]), 0.0)
    share_sum, mass_total = lax.psum((jnp.sum(weights_exp, axis=1), mass_local), "context")
    probability = weights_exp / share_sum[:, None]
    target = row_mass / mass_total[:, None]
    slopes = loss_scale * (probability - target)
    slope_blocks = slopes.reshape(own_rows, block_total, block_keys).transpose(1, 0, 2)

    def back_step(query_grad, inputs):
        key_block, slope_block = inputs
        products = block_dots(key_block)
        terms = jnp.where(
            products > 0, slope_block[:, None, :] * index_weight[:, :, None] * index_scale, 0.0
        )
        terms = terms.astype(jnp.bfloat16).reshape(own_rows * heads_count, key_block.shape[0])
        query_grad = query_grad + jnp.dot(terms, key_block, preferred_element_type=jnp.float32)
        key_grad = lax.dot_general(
            terms, flat_query, (((0,), (0,)), ((), ())), preferred_element_type=jnp.float32
        )
        return (query_grad, key_grad)

    start_grad = jnp.zeros((own_rows * heads_count, width), jnp.float32)
    query_grad, key_grads = lax.scan(back_step, start_grad, (key_blocks, slope_blocks))
    query_grad = query_grad.reshape(own_rows, heads_count, width)
    key_grad = key_grads.reshape(key_count, width)
    out_query = lax.psum_scatter(query_grad, "context", scatter_dimension=1, tiled=True)
    out_key = lax.psum_scatter(key_grad, "heads", scatter_dimension=0, tiled=True)
    return (out_query, out_key)


def solution(mesh):
    placed = (
        P("context", "heads", None),
        P("context", None),
        P(None, "heads"),
        P(),
        P("heads", None, None),
        P("context", None),
        P("heads", None),
    )
    return jax.shard_map(
        on_device,
        mesh=mesh,
        in_specs=placed,
        out_specs=(P("heads", "context", None), P(("context", "heads"), None)),
        check_vma=False,
    )
```

profile of v0, /device:TPU:2, one launch (start us, length us, event | category | flops | bytes accessed | tf_op | source)
XLA Modules:
  0.0 374.9 jit_solution(15053279912884742428)
XLA Ops:
  7.2 0.7 all-gather.2.cloned.1.call-update
  8.0 0.8 reshape.139
  8.8 0.8 dynamic_slice.31
  9.5 0.8 copy.25
  10.3 0.8 mul.63
  11.1 41.8 %all-gather.2.cloned.1.call-done = bf16[256,8,576]{2,1,0:T(8,128)(2,1)} async-done(((bf16[16,8,576]{2,1,0:T(8,128)(2,1)}), bf16[256,8,576]{2,1,0:T(8,128)(2,1)}) %all-gather.2.cloned.1.call-update) | async-done | bytes 2359312 | tf_op jit(solution)/shard_map/all_gather | solution.py:44
  52.9 22.9 %while.36 = (s32[]{:T(128)}, f32[4,64,2048]{2,1,0:T(8,128)}, s32[4,64]{1,0:T(4,128)S(1)}, bf16[4,64,8,576]{3,2,1,0:T(8,128)(2,1)}, bf16[2048,576]{0,1:T(8,128)(2...) while((s32[]{:T(128)}, f32[4,64,2048]{2,1,0:T(8,128)}, s32[4,64]{1,0:T(4,128)S(1)}, ...), condition=%wide.region_8.9_spmd.clone, body=%wide.region_6.8_spmd.clone.sunk | while | flops 1211238400 | bytes 4611937 | solution.py:27
  52.9 4.8 %exponential_reduce_fusion.2 = f32[64,2048]{1,0:T(8,128)S(1)} fusion(bf16[2048,576]{0,1:T(8,128)(2,1)} %get-tuple-element.382, f32[64,8]{1,0:T(8,128)S(1)} %dynamic-slice_bitcast_fusion.5, bf16[4,64,8,576]{3,2,1,0:T(8,128)(2,1)} %get-tuple-element.381, s32[]{:T(128)} %get-tuple-element.370), kind=kOutput, calls=%fused_computation.7.clone.1 | convolution fusion | flops 1210974208 | bytes 3541504 | tf_op jit(solution)/shard_map/while/body/eval_jaxpr/rhd,sd->rhs/dot_general | solution.py:21
  57.7 0.9 fusion.60
  58.6 4.8 %exponential_reduce_fusion.2 = f32[64,2048]{1,0:T(8,128)S(1)} fusion(bf16[2048,576]{0,1:T(8,128)(2,1)} %get-tuple-element.382, f32[64,8]{1,0:T(8,128)S(1)} %dynamic-slice_bitcast_fusion.5, bf16[4,64,8,576]{3,2,1,0:T(8,128)(2,1)} %get-tuple-element.381, s32[]{:T(128)} %get-tuple-element.370), kind=kOutput, calls=%fused_computation.7.clone.1 | convolution fusion | flops 1210974208 | bytes 3541504 | tf_op jit(solution)/shard_map/while/body/eval_jaxpr/rhd,sd->rhs/dot_general | solution.py:21
  63.4 0.9 fusion.60
  64.3 4.8 %exponential_reduce_fusion.2 = f32[64,2048]{1,0:T(8,128)S(1)} fusion(bf16[2048,576]{0,1:T(8,128)(2,1)} %get-tuple-element.382, f32[64,8]{1,0:T(8,128)S(1)} %dynamic-slice_bitcast_fusion.5, bf16[4,64,8,576]{3,2,1,0:T(8,128)(2,1)} %get-tuple-element.381, s32[]{:T(128)} %get-tuple-element.370), kind=kOutput, calls=%fused_computation.7.clone.1 | convolution fusion | flops 1210974208 | bytes 3541504 | tf_op jit(solution)/shard_map/while/body/eval_jaxpr/rhd,sd->rhs/dot_general | solution.py:21
  69.1 0.9 fusion.60
  70.0 4.8 %exponential_reduce_fusion.2 = f32[64,2048]{1,0:T(8,128)S(1)} fusion(bf16[2048,576]{0,1:T(8,128)(2,1)} %get-tuple-element.382, f32[64,8]{1,0:T(8,128)S(1)} %dynamic-slice_bitcast_fusion.5, bf16[4,64,8,576]{3,2,1,0:T(8,128)(2,1)} %get-tuple-element.381, s32[]{:T(128)} %get-tuple-element.370), kind=kOutput, calls=%fused_computation.7.clone.1 | convolution fusion | flops 1210974208 | bytes 3541504 | tf_op jit(solution)/shard_map/while/body/eval_jaxpr/rhd,sd->rhs/dot_general | solution.py:21
  74.8 0.9 fusion.60
  75.8 0.9 copy-done
  76.9 19.8 %while.35 = (s32[]{:T(128)}, f32[4,16,512]{2,1,0:T(8,128)S(1)}, bf16[4,512,128]{2,1,0:T(8,128)(2,1)S(1)}, bf16[1024,128]{1,0:T(8,128)(2,1)S(1)}, f32[16,64]{1,0:T(8,128)S(1)}, /*index=5*/s32[]{:T(128)}) while((s32[]{:T(128)}, f32[4,16,512]{2,1,0:T(8,128)S(1)}, bf16[4,512,128]{2,1,0:T(8,128)(2,1)S(1)}, bf16[1024,128]{1,0:T(8,128)(2,1)S(1)}, ...), condition=%wide.region_1.2_spmd, body=%wide.region_0.1_spmd.sunk | while | flops 141041664 | bytes 8884301 | solution.py:79
  76.9 1.8 maximum_bitcast_fusion.2
  78.7 1.9 copy.41
  80.6 1.2 fusion.56
  81.8 1.8 maximum_bitcast_fusion.2
  83.6 1.9 copy.41
  85.6 1.2 fusion.56
  86.8 1.8 maximum_bitcast_fusion.2
  88.6 1.9 copy.41
  90.5 1.2 fusion.56
  91.8 1.8 maximum_bitcast_fusion.2
  93.6 1.9 copy.41
  95.5 1.2 fusion.56
  97.0 24.9 %pmax.7 = f32[16]{0:T(128)S(1)} all-reduce(f32[16]{0:T(128)S(1)} %fusion.18), channel_id=1, replica_groups=mesh['context'=16,'heads'=16] {'context'}, use_global_device_ids=true, to_apply=%region_3.4 | all-reduce | flops 16 | bytes 128 | tf_op jit(solution)/shard_map/pmax | solution.py:82
  122.1 53.3 %all-reduce.3.cloned.1.call-done = f32[256,2048]{1,0:T(8,128)} async-done(((f32[256,2048]{1,0:T(8,128)}), f32[256,2048]{1,0:T(8,128)}) %all-reduce.3.cloned.1.call-update) | async-done | bytes 2097168 | tf_op jit(solution)/shard_map/psum | solution.py:50
  175.4 1.0 dynamic-slice_reduce_fusion
  176.4 24.2 %all-reduce = (f32[16]{0:T(128)S(1)}, f32[16]{0:T(128)S(1)}) all-reduce(f32[16]{0:T(128)S(1)} %dynamic-slice_reduce_fusion, f32[16]{0:T(128)S(1)} %fusion.19), channel_id=1, replica_groups=mesh['context'=16,'heads'=16] {'context'}, use_global_device_ids=true, to_apply=%region_11.12 | all-reduce | flops 32 | bytes 256 | tf_op jit(solution)/shard_map/psum | solution.py:84
  200.6 1.0 subtract_multiply_fusion
  201.6 0.7 copy.35
  202.3 26.9 %while.37 = (s32[]{:T(128)}, f32[1024,128]{1,0:T(8,128)S(1)}, f32[4,512,128]{2,1,0:T(8,128)}, bf16[4,512,128]{2,1,0:T(8,128)(2,1)S(1)}, bf16[1024,128]{1,0:T(8,1...) while((s32[]{:T(128)}, f32[1024,128]{1,0:T(8,128)S(1)}, ...), condition=%wide.wide.region_13.14_spmd.clone, body=%wide.wide.region_12.13_spmd.clone.sunk | while | flops 405536768 | bytes 13734523 | solution.py:104
  202.3 0.8 dynamic-slice_bitcast_fusion.6
  203.1 0.2 mul.80
  203.3 1.8 copy.42
  205.2 2.1 select_convert_fusion.3
  207.3 0.6 convolution_add_fusion.3
  207.9 1.1 fusion.67
  209.0 0.8 dynamic-slice_bitcast_fusion.6
  209.8 0.2 mul.80
  210.0 1.8 copy.42
  211.9 2.1 select_convert_fusion.3
  214.0 0.6 convolution_add_fusion.3
  214.6 1.1 fusion.67
  215.8 0.8 dynamic-slice_bitcast_fusion.6
  216.5 0.2 mul.80
  216.8 1.8 copy.42
  218.6 2.1 select_convert_fusion.3
  220.7 0.6 convolution_add_fusion.3
  221.3 1.1 fusion.67
  222.5 0.8 dynamic-slice_bitcast_fusion.6
  223.5 1.8 copy.42
  225.3 2.1 select_convert_fusion.3
  227.4 0.6 convolution_add_fusion.3
  228.1 1.2 fusion.67
  229.2 1.1 copy.27
  230.4 0.5 reduce-scatter.5.cloned.1.call-update
  231.0 56.1 %reduce-scatter.3.cloned.1.call-done = f32[16,4,128]{2,0,1:T(8,128)} async-done(((f32[16,64,128]{2,0,1:T(8,128)}), f32[16,4,128]{2,0,1:T(8,128)}) %reduce-scatter.3.cloned.1.call-update) | async-done | bytes 32784 | tf_op jit(solution)/shard_map/reduce_scatter | solution.py:107
  287.1 1.4 copy.28
  288.5 79.9 %reduce-scatter.5.cloned.1.call-done = f32[128,128]{1,0:T(8,128)} async-done(((f32[2048,128]{1,0:T(8,128)}), f32[128,128]{1,0:T(8,128)}) %reduce-scatter.5.cloned.1.call-update) | async-done | bytes 65552 | tf_op jit(solution)/shard_map/reduce_scatter | solution.py:108
  (37 shorter events, 1.2 us)
Async XLA Ops:
  7.2 45.7 %all-gather.2.cloned.1.call-start = ((), (), s32[]{:S(2)}) async-start(), calls=%async_computation.2 | async-start | bytes 2785280 | tf_op jit(solution)/shard_map/all_gather | solution.py:44
  7.9 167.5 %all-reduce.3.cloned.1.call-start = ((), (), s32[]{:S(2)}) async-start(), calls=%async_computation.3 | async-start | bytes 4194304 | tf_op jit(solution)/shard_map/psum | solution.py:50
  75.8 0.9 copy-start
  75.8 1.1 copy-start.1
  75.8 1.1 copy-start.2
  75.8 211.3 %reduce-scatter.3.cloned.1.call-start = ((), (), s32[]{:S(2)}) async-start(), calls=%async_computation.4 | async-start | bytes 557056 | tf_op jit(solution)/shard_map/reduce_scatter | solution.py:107
  230.4 138.0 %reduce-scatter.5.cloned.1.call-start = ((), (), s32[]{:S(2)}) async-start(), calls=%async_computation.5 | async-start | bytes 1114112 | tf_op jit(solution)/shard_map/reduce_scatter | solution.py:108
Sparse Core Ops, SparseCore 0:
  9.8 43.0 all-gather.1
  75.9 99.3 all-reduce.2
  230.5 56.5 reduce-scatter.2
  291.0 77.3 reduce-scatter.4
where the time goes:
time: 376 us; the launch traced here: 375 us
  waiting for transfers between devices  232 us (62%)
  blocking collectives  49.1 us (13%)
  matrix products  46.5 us (12%)
  local copies, waits for them, and re-layouts  26.4 us (7%)
  between operations  13.8 us (4%)
  other arithmetic  6.2 us (2%)
    reduce_scatter x1, waiting for transfers between devices, on_device(): lax.psum_scatter(key_grad, 'heads', scatter_dimension=0, tiled=True)  79.9 us
    reduce_scatter x1, waiting for transfers between devices, on_device(): lax.psum_scatter(query_grad, 'context', scatter_dimension=1, tiled=True)  56.1 us
    psum x1, waiting for transfers between devices, on_device(): summed_mass = lax.psum(partial_mass, 'heads')  53.3 us
    all_gather x1, waiting for transfers between devices, on_device(): lax.all_gather(main_query, 'context', axis=0, tiled=True)  41.8 us
    pmax x1, blocking collectives, on_device(): top = lax.pmax(local_top, 'context')  24.9 us
    psum x1, blocking collectives, on_device(): lax.psum((jnp.sum(weights_exp, axis=1), mass_local), 'context')  24.2 us
    dot_general x4, matrix products, one_block(): jnp.einsum('rhd,sd->rhs', query_block, latent, preferred_element_type=jnp...  19 us
    dot_general x8, matrix products, block_dots(): lax.dot_general(flat_query, key_block, (((1,), (1,)), ((), ())), preferre...  15.5 us
  transfers between devices with their start and end apart: 4, of which 4 were waited for; matrix products, arithmetic and copies ran while one was open for 7% of the time, Pallas kernels for 0%

commit v1 on v0

--- a/solution.py
+++ b/solution.py
@@ -47,7 +47,8 @@
         latent_keys,
         first_key,
     )
-    summed_mass = lax.psum(partial_mass, "heads")
+    formed = lax.all_gather(partial_mass, "heads")
+    summed_mass = jnp.sum(formed, 0)
     row_mass = lax.dynamic_slice_in_dim(summed_mass, row_first, own_rows, 0)
     own_len = lax.dynamic_slice_in_dim(lengths, row_first, own_rows, 0)
     visible = (first_key + jnp.arange(key_count, dtype=jnp.int32))[None, :] < own_len[:, None]

time: 376 us -> 485 us (1.29)
  waiting for transfers between devices: 232 us -> 330 us
  other arithmetic: 6.2 us -> 18.6 us
    all_gather x0 -> x1, waiting for transfers between devices: none -> 151 us  [on_device(): formed = lax.all_gather(partial_mass, 'heads')]
    psum x1 -> x0, waiting for transfers between devices: 53.3 us -> none  [on_device(): summed_mass = lax.psum(partial_mass, 'heads')]
    reduce_sum x0 -> x1, other arithmetic: none -> 11.8 us  [on_device(): summed_mass = jnp.sum(formed, 0)]
  transfers between devices with their start and end apart: 4 -> 4, of which waited for: 4 -> 4; matrix products, arithmetic and copies ran while one was open for 7% -> 5% of each run, Pallas kernels for 0% -> 0%
where the time goes in v1:
time: 485 us; the launch traced here: 484 us
  waiting for transfers between devices  330 us (68%)
  blocking collectives  53.5 us (11%)
  matrix products  46.4 us (10%)
  local copies, waits for them, and re-layouts  21.6 us (4%)
  other arithmetic  18.6 us (4%)
  between operations  13.9 us (3%)
    all_gather x1, waiting for transfers between devices, on_device(): formed = lax.all_gather(partial_mass, 'heads')  151 us
    reduce_scatter x1, waiting for transfers between devices, on_device(): lax.psum_scatter(key_grad, 'heads', scatter_dimension=0, tiled=True)  79.8 us
    reduce_scatter x1, waiting for transfers between devices, on_device(): lax.psum_scatter(query_grad, 'context', scatter_dimension=1, tiled=True)  54.1 us
    all_gather x1, waiting for transfers between devices, on_device(): lax.all_gather(main_query, 'context', axis=0, tiled=True)  43.3 us
    psum x1, blocking collectives, on_device(): lax.psum((jnp.sum(weights_exp, axis=1), mass_local), 'context')  26.8 us
    pmax x1, blocking collectives, on_device(): top = lax.pmax(local_top, 'context')  26.7 us
    dot_general x4, matrix products, one_block(): jnp.einsum('rhd,sd->rhs', query_block, latent, preferred_element_type=jnp...  18.9 us
    dot_general x8, matrix products, block_dots(): lax.dot_general(flat_query, key_block, (((1,), (1,)), ((), ())), preferre...  15.6 us
  transfers between devices with their start and end apart: 4, of which 4 were waited for; matrix products, arithmetic and copies ran while one was open for 5% of the time, Pallas kernels for 0%

profile of v1, /device:TPU:2, one launch (start us, length us, event | category | flops | bytes accessed | tf_op | source)
XLA Modules:
  0.0 484.1 jit_solution(8940112433173455282)
XLA Ops:
  7.2 0.7 all-gather.3.cloned.1.call-update
  8.0 0.8 copy.24
  8.8 0.8 reshape.136
  9.6 43.3 %all-gather.3.cloned.1.call-done = bf16[256,8,576]{2,1,0:T(8,128)(2,1)} async-done(((bf16[16,8,576]{2,1,0:T(8,128)(2,1)}), bf16[256,8,576]{2,1,0:T(8,128)(2,1)}) %all-gather.3.cloned.1.call-update) | async-done | bytes 2359312 | tf_op jit(solution)/shard_map/all_gather | solution.py:44
  52.9 22.7 %while.36 = (s32[]{:T(128)}, f32[4,64,2048]{2,1,0:T(8,128)}, s32[4,64]{1,0:T(4,128)S(1)}, bf16[4,64,8,576]{3,2,1,0:T(8,128)(2,1)}, bf16[2048,576]{0,1:T(8,128)(2...) while((s32[]{:T(128)}, f32[4,64,2048]{2,1,0:T(8,128)}, s32[4,64]{1,0:T(4,128)S(1)}, ...), condition=%wide.region_8.9_spmd.clone, body=%wide.region_6.8_spmd.clone.sunk | while | flops 1211238400 | bytes 4611937 | solution.py:27
  52.9 4.7 exponential_reduce_fusion.2
  57.6 0.9 fusion.60
  58.5 4.7 exponential_reduce_fusion.2
  63.3 0.9 fusion.60
  64.2 4.7 exponential_reduce_fusion.2
  69.0 0.9 fusion.60
  69.9 4.7 exponential_reduce_fusion.2
  74.7 0.9 fusion.60
  75.7 0.6 copy-done.5
  76.4 0.2 copy-done
  76.5 0.2 copy-done.1
  76.7 20.1 %while.35 = (s32[]{:T(128)}, f32[4,16,512]{2,1,0:T(8,128)S(1)}, bf16[4,512,128]{2,1,0:T(8,128)(2,1)S(1)}, bf16[1024,128]{1,0:T(8,128)(2,1)S(1)}, f32[16,64]{1,0:T(8,128)S(1)}, /*index=5*/s32[]{:T(128)}) while((s32[]{:T(128)}, f32[4,16,512]{2,1,0:T(8,128)S(1)}, bf16[4,512,128]{2,1,0:T(8,128)(2,1)S(1)}, bf16[1024,128]{1,0:T(8,128)(2,1)S(1)}, ...), condition=%wide.region_1.2_spmd, body=%wide.region_0.1_spmd.sunk | while | flops 141041664 | bytes 8884301 | solution.py:80
  76.7 1.8 maximum_bitcast_fusion.2
  78.5 1.9 copy.40
  80.4 1.2 fusion.56
  81.7 1.8 maximum_bitcast_fusion.2
  83.5 1.9 copy.40
  85.4 1.2 fusion.56
  86.6 1.8 maximum_bitcast_fusion.2
  88.4 2.1 copy.40
  90.6 1.2 fusion.56
  91.8 1.8 maximum_bitcast_fusion.2
  93.6 1.9 copy.40
  95.6 1.2 fusion.56
  96.8 0.2 fusion.18
  97.0 26.7 %pmax.7 = f32[16]{0:T(128)S(1)} all-reduce(f32[16]{0:T(128)S(1)} %fusion.18), channel_id=1, replica_groups=mesh['context'=16,'heads'=16] {'context'}, use_global_device_ids=true, to_apply=%region_3.4 | all-reduce | flops 16 | bytes 128 | tf_op jit(solution)/shard_map/pmax | solution.py:83
  123.7 0.6 iota_add_fusion.1
  124.3 0.8 fusion.19
  125.1 151.2 %all-gather.5.cloned.1.call-done = f32[16,256,2048]{2,1,0:T(8,128)} async-done(((f32[1,256,2048]{2,1,0:T(8,128)}), f32[16,256,2048]{2,1,0:T(8,128)}) %all-gather.5.cloned.1.call-update) | async-done | bytes 33554448 | tf_op jit(solution)/shard_map/all_gather | solution.py:50
  276.3 11.8 %reduce_sum.39 = f32[256,2048]{1,0:T(8,128)S(1)} reduce(f32[16,256,2048]{2,1,0:T(8,128)} %all-gather.5.cloned.1.call-done, f32[]{:T(128)} %constant.44.clone.1), dimensions={0}, to_apply=%region_9.10 | reduce | flops 7864320 | bytes 35651588 | tf_op jit(solution)/shard_map/reduce_sum | solution.py:51
  288.1 0.7 dynamic-slice_reduce_fusion
  288.8 26.8 %all-reduce = (f32[16]{0:T(128)}, f32[16]{0:T(128)}) all-reduce(f32[16]{0:T(128)} %dynamic-slice_reduce_fusion, f32[16]{0:T(128)} %fusion.19), channel_id=1, replica_groups=mesh['context'=16,'heads'=16] {'context'}, use_global_device_ids=true, to_apply=%region_11.12 | all-reduce | flops 32 | bytes 256 | tf_op jit(solution)/shard_map/psum | solution.py:85
  315.6 0.8 subtract_multiply_fusion
  316.4 24.2 %while.37 = (s32[]{:T(128)}, f32[1024,128]{1,0:T(8,128)S(1)}, f32[4,512,128]{2,1,0:T(8,128)}, bf16[4,512,128]{2,1,0:T(8,128)(2,1)S(1)}, bf16[1024,128]{1,0:T(8,1...) while((s32[]{:T(128)}, f32[1024,128]{1,0:T(8,128)S(1)}, ...), condition=%wide.wide.region_13.14_spmd.clone, body=%wide.wide.region_12.13_spmd.clone.sunk | while | flops 405536768 | bytes 13734523 | solution.py:105
  316.4 0.3 mul.80
  316.7 1.9 copy.41
  318.6 2.1 select_convert_fusion.3
  320.7 0.6 convolution_add_fusion.3
  321.3 1.2 fusion.67
  322.5 0.3 mul.80
  322.7 1.9 copy.41
  324.6 2.1 select_convert_fusion.3
  326.7 0.6 convolution_add_fusion.3
  327.4 1.1 fusion.67
  328.5 0.3 mul.80
  328.8 1.9 copy.41
  330.6 2.1 select_convert_fusion.3
  332.7 0.6 convolution_add_fusion.3
  333.4 1.1 fusion.67
  334.5 0.3 mul.80
  334.8 1.9 copy.41
  336.7 2.1 select_convert_fusion.3
  338.8 0.6 convolution_add_fusion.3
  339.4 1.2 fusion.67
  340.6 1.1 copy.26
  341.7 0.5 reduce-scatter.5.cloned.1.call-update
  342.3 54.1 %reduce-scatter.3.cloned.1.call-done = f32[16,4,128]{2,0,1:T(8,128)} async-done(((f32[16,64,128]{2,0,1:T(8,128)}), f32[16,4,128]{2,0,1:T(8,128)}) %reduce-scatter.3.cloned.1.call-update) | async-done | bytes 32784 | tf_op jit(solution)/shard_map/reduce_scatter | solution.py:108
  396.4 1.4 copy.27
  397.8 79.8 %reduce-scatter.5.cloned.1.call-done = f32[128,128]{1,0:T(8,128)} async-done(((f32[2048,128]{1,0:T(8,128)}), f32[128,128]{1,0:T(8,128)}) %reduce-scatter.5.cloned.1.call-update) | async-done | bytes 65552 | tf_op jit(solution)/shard_map/reduce_scatter | solution.py:109
  (44 shorter events, 0.5 us)
Async XLA Ops:
  7.2 45.7 %all-gather.3.cloned.1.call-start = ((), (), s32[]{:S(2)}) async-start(), calls=%async_computation.2 | async-start | bytes 2785280 | tf_op jit(solution)/shard_map/all_gather | solution.py:44
  7.9 268.4 %all-gather.5.cloned.1.call-start = ((), (), s32[]{:S(2)}) async-start(), calls=%async_computation.3 | async-start | bytes 35651584 | tf_op jit(solution)/shard_map/all_gather | solution.py:50
  75.6 0.7 copy-start.5
  75.6 0.8 copy-start.2
  75.6 1.0 copy-start
  75.6 1.1 copy-start.1
  75.6 320.8 %reduce-scatter.3.cloned.1.call-start = ((), (), s32[]{:S(2)}) async-start(), calls=%async_computation.4 | async-start | bytes 557056 | tf_op jit(solution)/shard_map/reduce_scatter | solution.py:108
  123.7 1.4 copy-start.4
  125.1 190.5 %copy-start.3 = (s32[2048]{0:T(1024)S(1)}, s32[2048]{0:T(1024)}, u32[]{:S(2)}) copy-start(s32[2048]{0:T(1024)} %iota_add_fusion.1) | copy-start | bytes 24580
  341.7 135.9 %reduce-scatter.5.cloned.1.call-start = ((), (), s32[]{:S(2)}) async-start(), calls=%async_computation.5 | async-start | bytes 1114112 | tf_op jit(solution)/shard_map/reduce_scatter | solution.py:109
Sparse Core Ops, SparseCore 0:
  9.8 43.0 all-gather.2
  75.7 200.5 all-gather.4
  341.8 54.5 reduce-scatter.2
  400.3 77.2 reduce-scatter.4
